TPU v7x, 32 devices: a whole 2x2x4 slice. The times are simulated.
32 devices in a mesh: row: 8 (over y, x, core), col: 4 (over z).
Axes of the slice: x: 2, y: 2, z: 4, core: 2. Of those that a mesh axis runs over, the one named last changes fastest.
Arguments:
- chol: bfloat16 [3, 6144, 2048], P(None, 'row', 'col'), may hold values from -0.67578125 to 0.67578125
- amps: bfloat16 [9, 2048, 2048], P(None, 'row', 'col'), may hold values from -0.19921875 to 0.19921875
- eps_occ: float32 [3], replicated, may hold values from -2 to -0.5
- eps_vir: float32 [2048], replicated, may hold values from 1 to 8
- pairs: int32 [9, 2], replicated, may hold values from 0 to 2, as said below
Outputs:
- residual: float32 [9, 2048, 2048], P(None, 'row', 'col')
Inputs may be any that keep to these rules, and one draw needn't show every extreme that they name: `pairs`: the rows list every ordered pair (i, j) of orbitals 0 to 2 exactly once.
All inputs are finite; a program needn't handle non-finite values.
Results may differ from a plain program's by a relative error of at most 0.0039.
Values may be sent and summed in bfloat16 or wider, within the bound.
A program may use at most 128 MiB of HBM per device.

v0:
```python
import jax
import jax.numpy as jnp
from jax import lax
from jax.sharding import PartitionSpec as P


def from_root(block, axis, source):
    block = jnp.where(lax.axis_index(axis) == source, block, jnp.zeros_like(block))
    return lax.psum(block, axis)


def per_device(chol, amps, eps_occ, eps_vir, pairs):
    row_index = lax.axis_index("row")
    col_index = lax.axis_index("col")
    occ = chol.shape[0]
    slabs = amps.shape[0]
    tile_rows = amps.shape[1]
    tile_cols = amps.shape[2]
    offset = row_index % 2 * tile_rows
    flat_pair = pairs[:, 0] * occ + pairs[:, 1]
    matches = (flat_pair[None, :] == jnp.arange(slabs, dtype=jnp.int32)[:, None]).astype(jnp.int32)
    slot = jnp.sum(matches * jnp.arange(slabs, dtype=jnp.int32)[None, :], axis=1)
    grid = jnp.take(amps, slot, axis=0).reshape(occ, occ, tile_rows, tile_cols)
    col_panels = lax.all_gather(chol, "row", axis=1, tiled=True)
    own_rows = lax.dynamic_slice_in_dim(col_panels, offset, tile_rows, 2)
    row_panels = from_root(own_rows, "col", row_index // 2)
    coulomb = lax.dot_general(
        row_panels, col_panels, (((1,), (1,)), ((), ())), preferred_element_type=jnp.float32
    )
    coulomb_b = coulomb.astype(jnp.bfloat16)
    left_rows = lax.all_gather(coulomb_b, "col", axis=3, tiled=True)
    left = left_rows
    dressing = lax.dot_general(
        left,
        lax.all_gather(grid, "row", axis=2, tiled=True),
        (((2, 3), (0, 2)), ((), ())),
        preferred_element_type=jnp.float32,
    )
    dressed = coulomb + dressing
    dressed_b = dressed.astype(jnp.bfloat16)
    amp_rows = lax.all_gather(grid, "col", axis=3, tiled=True)
    left = amp_rows
    quadratic = lax.dot_general(
        left,
        lax.all_gather(dressed_b, "row", axis=1, tiled=True),
        (((1, 3), (0, 1)), ((), ())),
        preferred_element_type=jnp.float32,
    )
    eps_rows = lax.dynamic_slice_in_dim(eps_vir, row_index * tile_rows, tile_rows, 0)
    eps_cols = lax.dynamic_slice_in_dim(eps_vir, col_index * tile_cols, tile_cols, 0)
    denom = (
        eps_rows[None, :, None, None]
        + eps_cols[None, None, None, :]
        - eps_occ[:, None, None, None]
        - eps_occ[None, None, :, None]
    )
    amp_float = jnp.transpose(grid, (0, 2, 1, 3)).astype(jnp.float32)
    result = denom * amp_float + dressed + quadratic
    ordered = jnp.transpose(result, (0, 2, 1, 3)).reshape(occ * occ, tile_rows, tile_cols)
    return jnp.take(ordered, flat_pair, axis=0)


def solution(mesh):
    placed = (P(None, "row", "col"), P(None, "row", "col"), P(), P(), P())
    return jax.shard_map(
        per_device, mesh=mesh, in_specs=placed, out_specs=P(None, "row", "col"), check_vma=False
    )
```

profile of v0, /device:TPU:0, one launch (start us, length us, event | category | flops | bytes accessed | tf_op | source)
XLA Modules:
  0.0 1017.2 jit_solution(9229886071944885983)
XLA Ops:
  6.5 0.0 copy-start
  6.5 0.0 all-gather.6.cloned.1.call-start
  6.5 0.7 all-gather.6.cloned.1.call-update
  7.3 0.0 all-reduce.2.cloned.1.call-start
  7.3 103.3 %all-gather.6.cloned.1.call-done = bf16[3,6144,512]{2,1,0:T(8,128)(2,1)} async-done(((bf16[3,768,512]{2,1,0:T(8,128)(2,1)}), bf16[3,6144,512]{2,1,0:T(8,128)(2,1)}) %all-gather.6.cloned.1.call-update) | async-done | bytes 18874384 | tf_op jit(solution)/shard_map/all_gather | solution.py:24
  110.6 8.8 dynamic-slice_select_fusion
  119.4 0.0 copy-start.3
  119.4 0.0 all-reduce.2.cloned.1.call-update
  119.5 0.0 all-gather.10.cloned.1.call-start
  119.5 0.6 copy-done.3
  120.1 0.1 select_reduce_fusion
  120.2 0.1 reduce_sum.14
  120.3 0.0 copy-done
  120.3 2.3 gather_fusion
  122.6 3.4 broadcast_select_fusion.1
  126.1 0.0 all-gather.10.cloned.1.call-update
  126.1 0.0 all-gather.8.cloned.1.call-start
  126.1 318.1 %all-reduce.2.cloned.1.call-done = bf16[3,6144,256]{2,1,0:T(8,128)(2,1)} async-done(((bf16[3,6144,256]{2,1,0:T(8,128)(2,1)}), bf16[3,6144,256]{2,1,0:T(8,128)(2,1)}) %all-reduce.2.cloned.1.call-update) | async-done | bytes 9437200 | tf_op jit(solution)/shard_map/psum | solution.py:9
  444.3 22.1 %fusion.21 = (bf16[3,256,3,512]{3,1,2,0:T(8,128)(2,1)}, f32[3,256,3,512]{3,1,2,0:T(8,128)}) fusion(bf16[3,6144,512]{2,1,0:T(8,128)(2,1)} %all-gather.6.cloned.1.call-done, bf16[3,6144,256]{2,1,0:T(8,128)(2,1)} %all-reduce.2.cloned.1.call-done), kind=kOutput, calls=%fused_computation.33 | convolution fusion | flops 14496694272 | bytes 35389440 | tf_op jit(solution)/shard_map/dot_general | solution.py:27
  466.4 0.0 all-gather.8.cloned.1.call-update
  466.4 0.0 all-gather.12.cloned.1.call-start
  466.4 0.5 all-gather.12.cloned.1.call-update
  467.0 0.2 all-gather.14.cloned.1.call-start
  467.2 76.6 %all-gather.10.cloned.1.call-done = bf16[3,3,2048,512]{3,2,1,0:T(8,128)(2,1)} async-done(((bf16[3,3,256,512]{3,2,1,0:T(8,128)(2,1)}), bf16[3,3,2048,512]{3,2,1,0:T(8,128)(2,1)}) %all-gather.10.cloned.1.call-update) | async-done | bytes 18874384 | tf_op jit(solution)/shard_map/all_gather | solution.py:35
  543.8 168.2 %all-gather.8.cloned.1.call-done = bf16[3,256,3,2048]{3,1,2,0:T(8,128)(2,1)} async-done(((bf16[3,256,3,512]{3,1,2,0:T(8,128)(2,1)}), bf16[3,256,3,2048]{3,1,2,0:T(8,128)(2,1)}) %all-gather.8.cloned.1.call-update) | async-done | bytes 9437200 | tf_op jit(solution)/shard_map/all_gather | solution.py:31
  712.0 0.0 copy-start.4
  712.0 22.5 %fusion.22 = (bf16[3,256,3,512]{3,1,2,0:T(8,128)(2,1)}, f32[3,256,3,512]{3,1,2,0:T(8,128)}) fusion(f32[3,256,3,512]{3,1,2,0:T(8,128)} %get-tuple-element.8, bf16[3,3,2048,512]{3,2,1,0:T(8,128)(2,1)} %all-gather.10.cloned.1.call-done, bf16[3,256,3,2048]{3,1,2,0:T(8,128)(2,1)} %all-gather.8.cloned.1.call-done), kind=kOutput, calls=%fused_computation.34 | convolution fusion | flops 14497873920 | bytes 40108032 | tf_op jit(solution)/shard_map/dot_general | solution.py:33
  734.5 0.0 copy-start.2
  734.5 0.0 all-gather.14.cloned.1.call-update
  734.5 0.9 dynamic_slice.9
  735.4 0.8 dynamic_slice.10
  736.2 0.1 broadcast_add_fusion
  736.3 0.0 copy-done.4
  736.3 1.5 broadcast_subtract_fusion
  737.8 140.5 %all-gather.12.cloned.1.call-done = bf16[3,3,256,2048]{3,2,1,0:T(8,128)(2,1)} async-done(((bf16[3,3,256,512]{3,2,1,0:T(8,128)(2,1)}), bf16[3,3,256,2048]{3,2,1,0:T(8,128)(2,1)}) %all-gather.12.cloned.1.call-update) | async-done | bytes 9437200 | tf_op jit(solution)/shard_map/all_gather | solution.py:41
  878.4 98.6 %all-gather.14.cloned.1.call-done = bf16[3,2048,3,512]{3,1,2,0:T(8,128)(2,1)} async-done(((bf16[3,256,3,512]{3,1,2,0:T(8,128)(2,1)}), bf16[3,2048,3,512]{3,1,2,0:T(8,128)(2,1)}) %all-gather.14.cloned.1.call-update) | async-done | bytes 18874384 | tf_op jit(solution)/shard_map/all_gather | solution.py:45
  976.9 0.0 copy-done.2
  976.9 22.7 %bitcast_add_fusion = f32[3,3,256,512]{3,2,1,0:T(8,128)} fusion(f32[3,256,3,512]{3,1,2,0:T(8,128)} %get-tuple-element.10, bf16[3,3,256,512]{3,2,1,0:T(8,128)(2,1)S(1)} %copy-done.2, f32[3]{0:T(128)S(1)} %copy-done.4, f32[3,256,512]{2,1,0:T(8,128)} %broadcast_subtract_fusion, bf16[3,2048,3,512]{3,1,2,0:T(8,128)(2,1)} %all-gather.14.cloned.1.call-done, ...), kind=kOutput, calls=%fused_computation.14 | convolution fusion | flops 14501412864 | bytes 41680908 | tf_op jit(solution)/shard_map/dot_general | solution.py:43
  999.6 5.3 gather_fusion.1
  1004.9 0.0 copy-start.1
  1004.9 5.4 broadcast_select_fusion
  1010.4 0.0 copy-done.1
  (6 shorter events, 0.0 us)
Async XLA Ops:
  6.5 113.8 %copy-start = (bf16[9,256,512]{2,1,0:T(8,128)(2,1)S(1)}, bf16[9,256,512]{2,1,0:T(8,128)(2,1)}, u32[]{:S(2)}) copy-start(bf16[9,256,512]{2,1,0:T(8,128)(2,1)} %param.6) | copy-start | bytes 7077892
  6.5 104.1 %all-gather.6.cloned.1.call-start = ((), (), s32[]{:S(2)}) async-start(), calls=%async_computation | async-start | bytes 21233664 | tf_op jit(solution)/shard_map/all_gather | solution.py:24
  7.3 437.0 %all-reduce.2.cloned.1.call-start = ((), (), s32[]{:S(2)}) async-start(), calls=%async_computation.1 | async-start | bytes 18874368 | tf_op jit(solution)/shard_map/psum | solution.py:9
  119.4 0.7 copy-start.3
  119.5 424.3 %all-gather.10.cloned.1.call-start = ((), (), s32[]{:S(2)}) async-start(), calls=%async_computation.3 | async-start | bytes 21233664 | tf_op jit(solution)/shard_map/all_gather | solution.py:35
  126.1 585.9 %all-gather.8.cloned.1.call-start = ((), (), s32[]{:S(2)}) async-start(), calls=%async_computation.2 | async-start | bytes 11796480 | tf_op jit(solution)/shard_map/all_gather | solution.py:31
  466.4 412.0 %all-gather.12.cloned.1.call-start = ((), (), s32[]{:S(2)}) async-start(), calls=%async_computation.4 | async-start | bytes 11796480 | tf_op jit(solution)/shard_map/all_gather | solution.py:41
  467.0 510.0 %all-gather.14.cloned.1.call-start = ((), (), s32[]{:S(2)}) async-start(), calls=%async_computation.5 | async-start | bytes 21233664 | tf_op jit(solution)/shard_map/all_gather | solution.py:45
  712.0 24.3 %copy-start.4 = (f32[3]{0:T(128)S(1)}, f32[3]{0:T(128)}, u32[]{:S(2)}) copy-start(f32[3]{0:T(128)} %param.7) | copy-start | bytes 40
  734.5 242.4 %copy-start.2 = (bf16[3,3,256,512]{3,2,1,0:T(8,128)(2,1)S(1)}, bf16[3,3,256,512]{3,2,1,0:T(8,128)(2,1)}, u32[]{:S(2)}) copy-start(bf16[3,3,256,512]{3,2,1,0:T(8,128)(2,1)} %broadcast_select_fusion.1) | copy-start | bytes 7077892
  1004.9 5.4 copy-start.1
Sparse Core Ops, SparseCore 0:
  9.2 101.3 all-gather.5
  119.6 324.6 all-reduce.1
  446.2 97.5 all-gather.9
  545.2 166.7 all-gather.7
  713.4 164.9 all-gather.11
  880.1 96.7 all-gather.13
where the time goes:
time: 1020 us
  waiting for transfers between devices  907 us (89%)
  matrix products  67.3 us (7%)
  other arithmetic  19.5 us (2%)
  between operations  13.5 us (1%)
    psum x1, waiting for transfers between devices, from_root(): return lax.psum(block, axis)  318 us
    all_gather x1, waiting for transfers between devices, per_device(): left_rows = lax.all_gather(coulomb_b, 'col', axis=3, tiled=True)  168 us
    all_gather x1, waiting for transfers between devices, per_device(): amp_rows = lax.all_gather(grid, 'col', axis=3, tiled=True)  141 us
    all_gather x1, waiting for transfers between devices, per_device(): col_panels = lax.all_gather(chol, 'row', axis=1, tiled=True)  103 us
    all_gather x1, waiting for transfers between devices, per_device(): lax.all_gather(dressed_b, 'row', axis=1, tiled=True)  98.6 us
    all_gather x1, waiting for transfers between devices, per_device(): lax.all_gather(grid, 'row', axis=2, tiled=True)  76.6 us
    dot_general x1, matrix products, per_device(): lax.dot_general(left, lax.all_gather(dressed_b, 'row', axis=1, tiled=True...  22.7 us
    dot_general x1, matrix products, per_device(): lax.dot_general(left, lax.all_gather(grid, 'row', axis=2, tiled=True), ((...  22.5 us
  transfers between devices with their start and end apart: 6, of which 6 were waited for; matrix products, arithmetic and copies ran while one was open for 5% of the time, Pallas kernels for 0%

commit v1 on v0

--- a/solution.py
+++ b/solution.py
@@ -2,6 +2,17 @@
 import jax.numpy as jnp
 from jax import lax
 from jax.sharding import PartitionSpec as P
+
+
+def collect(value, axis, dim):
+    ways = lax.axis_size(axis)
+    pieces = [value]
+    for far in range(1, ways):
+        pieces.append(
+            lax.ppermute(pieces[far - 1], axis, [(d, (d - 1) % ways) for d in range(ways)])
+        )
+    line = jnp.concatenate(pieces, axis=dim)
+    return jnp.roll(line, lax.axis_index(axis) * value.shape[dim], axis=dim)
 
 
 def from_root(block, axis, source):
@@ -38,7 +49,7 @@
     )
     dressed = coulomb + dressing
     dressed_b = dressed.astype(jnp.bfloat16)
-    amp_rows = lax.all_gather(grid, "col", axis=3, tiled=True)
+    amp_rows = collect(grid, "col", 3)
     left = amp_rows
     quadratic = lax.dot_general(
         left,

time: 1020 us -> 949 us (0.930)
  waiting for transfers between devices: 907 us -> 809 us
  local copies, waits for them, and re-layouts: 9.96 us -> 31.4 us
    ppermute x0 -> x3, waiting for transfers between devices: none -> 143 us  [collect(): lax.ppermute(pieces[far - 1], axis, [(d, (d - 1) % ways) for d in range(w...]
    all_gather x1 -> x0, waiting for transfers between devices: 141 us -> none  [per_device(): amp_rows = lax.all_gather(grid, 'col', axis=3, tiled=True)]
    all_gather x1, waiting for transfers between devices: 98.6 us -> 0.01 us  [per_device(): lax.all_gather(dressed_b, 'row', axis=1, tiled=True)]
    unnamed x10 -> x20, local copies, waits for them, and re-layouts: 0.62 us -> 18.9 us
  transfers between devices with their start and end apart: 6 -> 8, of which waited for: 6 -> 7; matrix products, arithmetic and copies ran while one was open for 5% -> 6% of each run, Pallas kernels for 0% -> 0%
where the time goes in v1:
time: 949 us; the launch traced here: 948 us
  waiting for transfers between devices  809 us (85%)
  matrix products  67.7 us (7%)
  local copies, waits for them, and re-layouts  31.4 us (3%)
  other arithmetic  20.8 us (2%)
  between operations  13.2 us (1%)
    psum x1, waiting for transfers between devices, from_root(): return lax.psum(block, axis)  317 us
    all_gather x1, waiting for transfers between devices, per_device(): left_rows = lax.all_gather(coulomb_b, 'col', axis=3, tiled=True)  168 us
    ppermute x3, waiting for transfers between devices, collect(): lax.ppermute(pieces[far - 1], axis, [(d, (d - 1) % ways) for d in range(w...  143 us
    all_gather x1, waiting for transfers between devices, per_device(): col_panels = lax.all_gather(chol, 'row', axis=1, tiled=True)  103 us
    all_gather x1, waiting for transfers between devices, per_device(): lax.all_gather(grid, 'row', axis=2, tiled=True)  77.3 us
    dot_general x1, matrix products, per_device(): lax.dot_general(left, lax.all_gather(dressed_b, 'row', axis=1, tiled=True...  22.8 us
    dot_general x1, matrix products, per_device(): lax.dot_general(left, lax.all_gather(grid, 'row', axis=2, tiled=True), ((...  22.7 us
    dot_general x1, matrix products, per_device(): lax.dot_general(row_panels, col_panels, (((1,), (1,)), ((), ())), preferr...  22.2 us
  transfers between devices with their start and end apart: 8, of which 7 were waited for; matrix products, arithmetic and copies ran while one was open for 6% of the time, Pallas kernels for 0%

profile of v1, /device:TPU:0, one launch (start us, length us, event | category | flops | bytes accessed | tf_op | source)
XLA Modules:
  0.0 948.4 jit_solution(12958245235492623053)
XLA Ops:
  6.5 0.0 copy-start
  6.5 0.0 all-gather.5.cloned.1.call-start
  6.5 0.7 all-gather.5.cloned.1.call-update
  7.3 0.0 all-reduce.2.cloned.1.call-start
  7.3 103.3 %all-gather.5.cloned.1.call-done = bf16[3,6144,512]{2,1,0:T(8,128)(2,1)} async-done(((bf16[3,768,512]{2,1,0:T(8,128)(2,1)}), bf16[3,6144,512]{2,1,0:T(8,128)(2,1)}) %all-gather.5.cloned.1.call-update) | async-done | bytes 18874384 | tf_op jit(solution)/shard_map/all_gather | solution.py:35
  110.6 8.8 dynamic-slice_select_fusion
  119.4 0.0 all-reduce.2.cloned.1.call-update
  119.5 0.0 all-gather.9.cloned.1.call-start
  119.5 0.6 copy-done.5
  120.1 0.1 select_reduce_fusion
  120.2 0.1 reduce_sum.14
  120.3 0.0 copy-done
  120.3 2.3 gather_fusion
  122.6 4.8 constant_dynamic-update-slice_fusion.7
  127.4 0.0 all-gather.9.cloned.1.call-update
  127.5 0.0 all-gather.7.cloned.1.call-start
  127.5 316.7 %all-reduce.2.cloned.1.call-done = bf16[3,6144,256]{2,1,0:T(8,128)(2,1)} async-done(((bf16[3,6144,256]{2,1,0:T(8,128)(2,1)}), bf16[3,6144,256]{2,1,0:T(8,128)(2,1)}) %all-reduce.2.cloned.1.call-update) | async-done | bytes 9437200 | tf_op jit(solution)/shard_map/psum | solution.py:20
  444.3 22.2 %fusion.23 = (bf16[3,256,3,512]{3,1,2,0:T(8,128)(2,1)}, f32[3,256,3,512]{3,1,2,0:T(8,128)}) fusion(bf16[3,6144,512]{2,1,0:T(8,128)(2,1)} %all-gather.5.cloned.1.call-done, bf16[3,6144,256]{2,1,0:T(8,128)(2,1)} %all-reduce.2.cloned.1.call-done), kind=kOutput, calls=%fused_computation.43 | convolution fusion | flops 14496694272 | bytes 35389440 | tf_op jit(solution)/shard_map/dot_general | solution.py:38
  466.4 0.0 all-gather.7.cloned.1.call-update
  466.4 0.0 all-gather.11.cloned.1.call-start
  466.5 77.3 %all-gather.9.cloned.1.call-done = bf16[3,3,2048,512]{3,2,1,0:T(8,128)(2,1)} async-done(((bf16[3,3,256,512]{3,2,1,0:T(8,128)(2,1)}), bf16[3,3,2048,512]{3,2,1,0:T(8,128)(2,1)}) %all-gather.9.cloned.1.call-update) | async-done | bytes 18874384 | tf_op jit(solution)/shard_map/all_gather | solution.py:46
  543.7 168.2 %all-gather.7.cloned.1.call-done = bf16[3,256,3,2048]{3,1,2,0:T(8,128)(2,1)} async-done(((bf16[3,256,3,512]{3,1,2,0:T(8,128)(2,1)}), bf16[3,256,3,2048]{3,1,2,0:T(8,128)(2,1)}) %all-gather.7.cloned.1.call-update) | async-done | bytes 9437200 | tf_op jit(solution)/shard_map/all_gather | solution.py:42
  712.0 22.7 %fusion.24 = (bf16[3,256,3,512]{3,1,2,0:T(8,128)(2,1)}, f32[3,256,3,512]{3,1,2,0:T(8,128)}) fusion(f32[3,256,3,512]{3,1,2,0:T(8,128)} %get-tuple-element.10, bf16[3,3,2048,512]{3,2,1,0:T(8,128)(2,1)} %all-gather.9.cloned.1.call-done, bf16[3,256,3,2048]{3,1,2,0:T(8,128)(2,1)} %all-gather.7.cloned.1.call-done), kind=kOutput, calls=%fused_computation.44 | convolution fusion | flops 14497873920 | bytes 40108032 | tf_op jit(solution)/shard_map/dot_general | solution.py:44
  734.7 0.0 all-gather.11.cloned.1.call-update
  734.7 0.0 copy-done.2
  734.7 0.3 collective-permute-start
  735.0 52.9 %collective-permute-done = bf16[3,3,256,512]{3,2,1,0:T(8,128)(2,1)S(1)} collective-permute-done((bf16[3,3,256,512]{3,2,1,0:T(8,128)(2,1)S(1)}, bf16[3,3,256,512]{3,2,1,0:T(8,128)(2,1)S(1)}, u32[]{:S(2)}, u32[]{:S(2)}) %collective-permute-start) | collective-permute-done | bytes 2359328 | tf_op jit(solution)/shard_map/ppermute | solution.py:12
  787.9 1.4 copy-done.3
  789.3 2.1 collective-permute-start.1
  791.4 50.4 %collective-permute-done.1 = bf16[3,3,256,512]{3,2,1,0:T(8,128)(2,1)} collective-permute-done((bf16[3,3,256,512]{3,2,1,0:T(8,128)(2,1)S(1)}, bf16[3,3,256,512]{3,2,1,0:T(8,128)(2,1)}, u32[]{:S(2)}, u32[]{:S(2)}) %collective-permute-start.1) | collective-permute-done | bytes 2359328 | tf_op jit(solution)/shard_map/ppermute | solution.py:12
  841.8 3.8 collective-permute-start.2
  845.6 0.8 dynamic_slice.13
  846.4 0.8 dynamic_slice.14
  847.1 0.1 broadcast_add_fusion
  847.3 0.0 copy-done.6
  847.3 1.4 broadcast_subtract_fusion
  848.7 3.5 constant_dynamic-update-slice_fusion.6
  852.1 3.4 constant_dynamic-update-slice_fusion.5
  855.5 39.4 %collective-permute-done.2 = bf16[3,3,256,512]{3,2,1,0:T(8,128)(2,1)} collective-permute-done((bf16[3,3,256,512]{3,2,1,0:T(8,128)(2,1)}, bf16[3,3,256,512]{3,2,1,0:T(8,128)(2,1)}, u32[]{:S(2)}, u32[]{:S(2)}) %collective-permute-start.2) | collective-permute-done | bytes 2359328 | tf_op jit(solution)/shard_map/ppermute | solution.py:12
  894.9 3.4 constant_dynamic-update-slice_fusion.4
  898.3 1.6 constant_dynamic-update-slice_fusion.3
  899.9 0.0 copy-done.4
  899.9 1.6 constant_dynamic-update-slice_fusion.2
  901.6 3.3 constant_dynamic-update-slice_fusion.1
  904.9 3.4 constant_dynamic-update-slice_fusion
  908.3 22.8 %bitcast_add_fusion = f32[3,3,256,512]{3,2,1,0:T(8,128)} fusion(f32[3,256,3,512]{3,1,2,0:T(8,128)} %get-tuple-element.12, bf16[3,3,256,512]{3,2,1,0:T(8,128)(2,1)S(1)} %copy-done.2, f32[3]{0:T(128)S(1)} %copy-done.6, f32[3,256,512]{2,1,0:T(8,128)} %broadcast_subtract_fusion, bf16[3,2048,3,512]{3,1,2,0:T(8,128)(2,1)} %all-gather.11.cloned.1.call-done, ...), kind=kOutput, calls=%fused_computation.15 | convolution fusion | flops 14501412864 | bytes 41680912 | tf_op jit(solution)/shard_map/dot_general | solution.py:54
  931.1 5.3 gather_fusion.1
  936.4 5.4 broadcast_select_fusion
  (14 shorter events, 0.1 us)
Async XLA Ops:
  6.5 113.8 %copy-start = (bf16[9,256,512]{2,1,0:T(8,128)(2,1)S(1)}, bf16[9,256,512]{2,1,0:T(8,128)(2,1)}, u32[]{:S(2)}) copy-start(bf16[9,256,512]{2,1,0:T(8,128)(2,1)} %param.6) | copy-start | bytes 7077892
  6.5 104.1 %all-gather.5.cloned.1.call-start = ((), (), s32[]{:S(2)}) async-start(), calls=%async_computation | async-start | bytes 21233664 | tf_op jit(solution)/shard_map/all_gather | solution.py:35
  7.3 437.0 %all-reduce.2.cloned.1.call-start = ((), (), s32[]{:S(2)}) async-start(), calls=%async_computation.1 | async-start | bytes 18874368 | tf_op jit(solution)/shard_map/psum | solution.py:20
  119.4 0.7 copy-start.5
  119.5 424.3 %all-gather.9.cloned.1.call-start = ((), (), s32[]{:S(2)}) async-start(), calls=%async_computation.3 | async-start | bytes 21233664 | tf_op jit(solution)/shard_map/all_gather | solution.py:46
  127.5 584.5 %all-gather.7.cloned.1.call-start = ((), (), s32[]{:S(2)}) async-start(), calls=%async_computation.2 | async-start | bytes 11796480 | tf_op jit(solution)/shard_map/all_gather | solution.py:42
  466.4 441.8 %all-gather.11.cloned.1.call-start = ((), (), s32[]{:S(2)}) async-start(), calls=%async_computation.4 | async-start | bytes 21233664 | tf_op jit(solution)/shard_map/all_gather | solution.py:56
  712.0 22.7 %copy-start.2 = (bf16[3,3,256,512]{3,2,1,0:T(8,128)(2,1)S(1)}, bf16[3,3,256,512]{3,2,1,0:T(8,128)(2,1)}, u32[]{:S(2)}) copy-start(bf16[3,3,256,512]{3,2,1,0:T(8,128)(2,1)} %get-tuple-element.8) | copy-start | bytes 7077892
  712.0 135.3 %copy-start.6 = (f32[3]{0:T(128)S(1)}, f32[3]{0:T(128)}, u32[]{:S(2)}) copy-start(f32[3]{0:T(128)} %param.7) | copy-start | bytes 40
  734.7 53.2 %collective-permute-start = (bf16[3,3,256,512]{3,2,1,0:T(8,128)(2,1)S(1)}, bf16[3,3,256,512]{3,2,1,0:T(8,128)(2,1)S(1)}, u32[]{:S(2)}, u32[]{:S(2)}) collective-permute-start(bf16[3,3,256,512]{3,2,1,0:T(8,128)(2,1)S(1)} %copy-done.2), channel_id=1, source_target_pairs={{0,3},{1,0},{2,1},{3,2},{4,7},{5,4},{6,5},{7,6},{8,11},{9,8},{10,9... | collective-permute-start | bytes 7077896 | tf_op jit(solution)/shard_map/ppermute | solution.py:12
  787.9 1.4 copy-start.3
  789.3 52.5 %collective-permute-start.1 = (bf16[3,3,256,512]{3,2,1,0:T(8,128)(2,1)S(1)}, bf16[3,3,256,512]{3,2,1,0:T(8,128)(2,1)}, u32[]{:S(2)}, u32[]{:S(2)}) collective-permute-start(bf16[3,3,256,512]{3,2,1,0:T(8,128)(2,1)S(1)} %collective-permute-done), channel_id=1, source_target_pairs={{0,3},{1,0},{2,1},{3,2},{4,7},{5,4},{6,5},{7,6},{8,11},{9,8},{10,9... | collective-permute-start | bytes 7077896 | tf_op jit(solution)/shard_map/ppermute | solution.py:12
  841.8 53.1 %collective-permute-start.2 = (bf16[3,3,256,512]{3,2,1,0:T(8,128)(2,1)}, bf16[3,3,256,512]{3,2,1,0:T(8,128)(2,1)}, u32[]{:S(2)}, u32[]{:S(2)}) collective-permute-start(bf16[3,3,256,512]{3,2,1,0:T(8,128)(2,1)} %collective-permute-done.1), channel_id=1, source_target_pairs={{0,3},{1,0},{2,1},{3,2},{4,7},{5,4},{6,5},{7,6},{8,11},{9,8},{10,9... | collective-permute-start | bytes 7077896 | tf_op jit(solution)/shard_map/ppermute | solution.py:12
  855.5 44.4 %copy-start.4 = (bf16[3,3,256,512]{3,2,1,0:T(8,128)(2,1)S(1)}, bf16[3,3,256,512]{3,2,1,0:T(8,128)(2,1)}, u32[]{:S(2)}) copy-start(bf16[3,3,256,512]{3,2,1,0:T(8,128)(2,1)} %copy-done.3) | copy-start | bytes 7077892
  936.4 5.4 copy-start.1
Sparse Core Ops, SparseCore 0:
  9.2 101.3 all-gather.4
  119.6 324.6 all-reduce.1
  446.2 97.5 all-gather.8
  545.2 166.7 all-gather.6
  734.8 96.7 all-gather.10
